TPU v7x, 512 devices: a whole 4x8x8 slice. The times are simulated.
512 devices in a mesh: ctx: 32 (over y, x), head: 16 (over z, core).
Axes of the slice: x: 4, y: 8, z: 8, core: 2. Of those that a mesh axis runs over, the one named last changes fastest.
Arguments:
- activations: bfloat16 [8192, 16384], P('ctx'), may hold values from -6 to 6
- w_query: bfloat16 [16384, 2048], P('ctx', 'head'), may hold values from -0.046875 to 0.046875
- w_keyval: bfloat16 [16384, 256], P('ctx', 'head'), may hold values from -0.046875 to 0.046875
- f_query: bfloat16 [16, 128, 128], P('head'), may hold values from -1 to 1
- f_key: bfloat16 [128, 128], replicated, may hold values from -1 to 1
- w_out: bfloat16 [2048, 16384], P('ctx', 'head'), may hold values from -0.75 to 0.75
Outputs:
- sublayer_out: bfloat16 [8192, 16384], P('ctx', 'head')
All inputs are finite; a program needn't handle non-finite values.
Results may differ from a plain program's by a relative error of at most 0.0086.
Values may be sent and summed in bfloat16 or wider, within the bound.
A program may use at most 64 MiB of HBM per device.

v0:
```python
import math
import jax
import jax.numpy as jnp
from jax import lax
from jax.sharding import PartitionSpec as P

WINDOW = 64


def from_behind(array, axis, by):
    size = lax.axis_size(axis)
    pairs = [(i, i + by) for i in range(size) if 0 <= i + by < size]
    return lax.ppermute(array, axis, pairs)


def prefix(array, axis, combine, identity):
    size, mine = (lax.axis_size(axis), lax.axis_index(axis))
    everything = jax.tree.map(
        lambda part, kind: lax.all_gather(part.astype(kind), axis),
        array,
        jax.tree.map(lambda a: jnp.bfloat16 if a.dtype == jnp.float32 else a.dtype, array),
    )
    start = jax.tree.map(
        lambda part, zero: jnp.broadcast_to(jnp.asarray(zero, part.dtype), part.shape),
        array,
        identity,
    )

    def step(k, before):
        reached = k < mine
        new = combine(
            before, jax.tree.map(lambda part, own: part[k].astype(own.dtype), everything, array)
        )
        return jax.tree.map(lambda a, b: jnp.where(reached, a, b), new, before)

    return lax.fori_loop(0, size, step, start)


def normalized(logits):
    rising = jnp.exp(logits)
    falling = jnp.exp(-logits)
    rising = rising / jnp.sum(rising, axis=-1, keepdims=True)
    falling = falling / jnp.sum(falling, axis=-1, keepdims=True)
    return jnp.concatenate([rising, falling], axis=-1).astype(jnp.bfloat16)


def state_of(features, values):
    matrix = jnp.einsum("nf,nc->fc", features, values, preferred_element_type=jnp.float32)
    totals = jnp.sum(features.astype(jnp.float32), axis=0)
    return (matrix, totals)


def add_states(earlier, later):
    return (earlier[0] + later[0], earlier[1] + later[1])


def per_device(activations, w_query, w_keyval, f_query, f_key, w_out):
    length = activations.shape[0]
    head_width = f_key.shape[0]
    local_heads = f_query.shape[0]
    columns = activations
    query_sum = jnp.dot(
        columns,
        lax.all_gather(w_query, "ctx", axis=0, tiled=True),
        preferred_element_type=jnp.float32,
    )
    pair_sum = jnp.dot(
        columns,
        lax.all_gather(w_keyval, "ctx", axis=0, tiled=True),
        preferred_element_type=jnp.float32,
    )
    queries = query_sum.astype(jnp.bfloat16)
    keyval = lax.all_gather(pair_sum.astype(jnp.bfloat16), "head", axis=1, tiled=True)
    border = from_behind(keyval[length - WINDOW :], "ctx", 1)
    extended = jnp.concatenate([border, keyval], axis=0)
    ext_keys = extended[:, :head_width]
    ext_vals = extended[:, head_width:]
    first_pos = lax.axis_index("ctx") * length - WINDOW
    present = first_pos + jnp.arange(length + WINDOW) >= 0
    ext_feats = normalized(jnp.dot(ext_keys, f_key, preferred_element_type=jnp.float32))
    ext_feats = jnp.where(present[:, None], ext_feats, jnp.zeros_like(ext_feats))
    contribution = state_of(ext_feats[:length], ext_vals[:length])
    identity = (
        jnp.zeros((2 * head_width, head_width), jnp.float32),
        jnp.zeros((2 * head_width,), jnp.float32),
    )
    matrix, totals = prefix(contribution, "ctx", add_states, identity)
    query_heads = queries.reshape(length, local_heads, head_width)
    query_feats = normalized(
        jnp.einsum("thc,hcf->htf", query_heads, f_query, preferred_element_type=jnp.float32)
    )
    offsets = jnp.arange(length)[:, None] + WINDOW - jnp.arange(length + WINDOW)[None, :]
    inside = (offsets >= 0) & (offsets < WINDOW) & present[None, :]
    beyond = (offsets >= WINDOW) & present[None, :]
    scale = 1.0 / math.sqrt(head_width)
    scores = (
        jnp.einsum("thc,kc->htk", query_heads, ext_keys, preferred_element_type=jnp.float32) * scale
    )
    near_w = jnp.where(inside[None], jnp.exp(scores), 0.0)
    far_w = jnp.where(
        beyond[None],
        jnp.einsum("htf,kf->htk", query_feats, ext_feats, preferred_element_type=jnp.float32),
        0.0,
    )
    weights = near_w + far_w
    feats_wide = query_feats.astype(jnp.float32)
    numerator = jnp.einsum(
        "htk,kc->htc", weights, ext_vals.astype(jnp.float32), precision=lax.Precision.HIGHEST
    )
    numerator = numerator + jnp.einsum(
        "htf,fc->htc", feats_wide, matrix, precision=lax.Precision.HIGHEST
    )
    denominator = jnp.sum(weights, axis=-1) + jnp.einsum(
        "htf,f->ht", feats_wide, totals, precision=lax.Precision.HIGHEST
    )
    attn_heads = (numerator / denominator[..., None]).astype(jnp.bfloat16)
    attn_rows = jnp.transpose(attn_heads, (1, 0, 2)).reshape(length, local_heads * head_width)
    all_heads = lax.all_gather(attn_rows, "head", axis=1, tiled=True)
    columns = all_heads
    projected = jnp.dot(
        columns,
        lax.all_gather(w_out, "ctx", axis=0, tiled=True),
        preferred_element_type=jnp.float32,
    )
    return projected.astype(jnp.bfloat16)


def solution(mesh):
    in_specs = (
        P("ctx", None),
        P("ctx", "head"),
        P("ctx", "head"),
        P("head", None, None),
        P(),
        P("ctx", "head"),
    )
    out_specs = P("ctx", "head")
    return jax.shard_map(
        per_device, mesh=mesh, in_specs=in_specs, out_specs=out_specs, check_vma=False
    )
```

profile of v0, /device:TPU:1, one launch (start us, length us, event | category | flops | bytes accessed | tf_op | source)
XLA Modules:
  0.0 402.4 jit_solution(3140013990136511824)
XLA Ops:
  6.5 39.9 %all_gather.27 = bf16[16384,16]{0,1:T(8,128)(2,1)S(1)} all-gather(bf16[512,16]{0,1:T(8,128)(2,1)} %param.10), channel_id=1, replica_groups=mesh['ctx'=32,'head'=16] {'ctx'}, dimensions={0}, use_global_device_ids=true | all-gather | bytes 540672 | tf_op jit(solution)/shard_map/all_gather | solution.py:69
  46.5 5.6 %convolution_convert_fusion.3 = bf16[256,16]{0,1:T(8,128)(2,1)S(1)} fusion(bf16[256,16384]{1,0:T(8,128)(2,1)} %param.8, bf16[16384,16]{0,1:T(8,128)(2,1)S(1)} %all_gather.27), kind=kOutput, calls=%fused_computation.16 | convolution fusion | flops 134221824 | bytes 8921088 | tf_op jit(solution)/shard_map/dot_general | solution.py:67
  52.1 35.5 %all_gather.28 = bf16[256,256]{0,1:T(8,128)(2,1)S(1)} all-gather(bf16[256,16]{0,1:T(8,128)(2,1)S(1)} %convolution_convert_fusion.3), channel_id=1, replica_groups=mesh['ctx'=32,'head'=16] {'head'}, dimensions={1}, use_global_device_ids=true | all-gather | bytes 139264 | tf_op jit(solution)/shard_map/all_gather | solution.py:73
  87.7 2.4 collective-permute-start
  90.1 1.3 collective-permute-done
  92.2 0.9 convolution_convert_fusion.1
  93.2 0.7 all-gather.8.cloned.1.call-update
  94.7 35.3 %all-gather.2 = bf16[32,1,256]{2,1,0:T(2,128)(2,1)S(1)} all-gather(bf16[1,1,256]{2,1,0:T(2,128)(2,1)S(1)} %reshape.161), channel_id=3, replica_groups=mesh['ctx'=32,'head'=16] {'ctx'}, dimensions={0}, use_global_device_ids=true | all-gather | bytes 16896 | tf_op jit(solution)/shard_map/all_gather | solution.py:19
  130.0 41.1 %all-gather.14.cloned.1.call-done = bf16[8192,128]{1,0:T(8,128)(2,1)} async-done(((bf16[256,128]{1,0:T(8,128)(2,1)}), bf16[8192,128]{1,0:T(8,128)(2,1)}) %all-gather.14.cloned.1.call-update) | async-done | bytes 2097168 | tf_op jit(solution)/shard_map/all_gather | solution.py:19
  171.1 30.8 %while.16 = (s32[]{:T(128)}, f32[256,128]{1,0:T(8,128)S(1)}, f32[256]{0:T(256)S(1)}, s32[]{:T(128)}, bf16[32,256,128]{2,1,0:T(8,128)(2,1)}, /*index=5*/bf16[32,256]{1,0:T(8,128)(2,1)S(1)}, s32[]{:T(128)}, s32[]{:T(128)}) while((s32[]{:T(128)}, f32[256,128]{1,0:T(8,128)S(1)}, f32[256]{0:T(256)S(1)}, s32[]{:T(128)}, ...), condition=%wide.region_6.7_spmd.clone, body=%wide.region_5.6_spmd.clone.sunk | while | flops 132100 | bytes 332403 | solution.py:36
  171.1 0.9 add_select_fusion.4
  172.1 0.9 add_select_fusion.4
  173.1 0.9 add_select_fusion.4
  174.0 0.9 add_select_fusion.4
  175.0 0.9 add_select_fusion.4
  175.9 0.9 add_select_fusion.4
  176.9 0.9 add_select_fusion.4
  177.9 0.9 add_select_fusion.4
  178.8 0.9 add_select_fusion.4
  179.8 0.9 add_select_fusion.4
  180.8 0.9 add_select_fusion.4
  181.7 0.9 add_select_fusion.4
  182.7 0.9 add_select_fusion.4
  183.7 0.9 add_select_fusion.4
  184.6 0.9 add_select_fusion.4
  185.6 0.9 add_select_fusion.4
  186.6 0.9 add_select_fusion.4
  187.5 0.9 add_select_fusion.4
  188.5 0.9 add_select_fusion.4
  189.4 0.9 add_select_fusion.4
  190.4 0.9 add_select_fusion.4
  191.4 0.9 add_select_fusion.4
  192.3 0.9 add_select_fusion.4
  193.3 0.9 add_select_fusion.4
  194.3 0.9 add_select_fusion.4
  195.2 0.9 add_select_fusion.4
  196.2 0.9 add_select_fusion.4
  197.2 0.9 add_select_fusion.4
  198.1 0.9 add_select_fusion.4
  199.1 0.9 add_select_fusion.4
  200.1 0.9 add_select_fusion.4
  201.0 0.9 add_select_fusion.4
  202.0 58.0 %all-gather.8.cloned.1.call-done = bf16[16384,128]{1,0:T(8,128)(2,1)} async-done(((bf16[512,128]{1,0:T(8,128)(2,1)}), bf16[16384,128]{1,0:T(8,128)(2,1)}) %all-gather.8.cloned.1.call-update) | async-done | bytes 4194320 | tf_op jit(solution)/shard_map/all_gather | solution.py:64
  260.0 6.9 %convolution_convert_fusion.2 = bf16[256,128]{1,0:T(8,128)(2,1)S(1)} fusion(bf16[256,16384]{1,0:T(8,128)(2,1)} %param.8, bf16[16384,128]{1,0:T(8,128)(2,1)} %all-gather.8.cloned.1.call-done), kind=kOutput, calls=%fused_computation.15 | convolution fusion | flops 1073774592 | bytes 12648448 | tf_op jit(solution)/shard_map/dot_general | solution.py:62
  268.3 1.2 fusion.6
  269.5 78.3 %all-gather.12.cloned.1.call-done = bf16[2048,1024]{1,0:T(8,128)(2,1)} async-done(((bf16[64,1024]{1,0:T(8,128)(2,1)}), bf16[2048,1024]{1,0:T(8,128)(2,1)}) %all-gather.12.cloned.1.call-update) | async-done | bytes 4194320 | tf_op jit(solution)/shard_map/all_gather | solution.py:122
  347.8 43.5 %all-gather.10.cloned.1.call-done = bf16[256,2048]{1,0:T(8,128)(2,1)} async-done(((bf16[256,128]{1,0:T(8,128)(2,1)}), bf16[256,2048]{1,0:T(8,128)(2,1)}) %all-gather.10.cloned.1.call-update) | async-done | bytes 1048592 | tf_op jit(solution)/shard_map/all_gather | solution.py:118
  391.3 4.6 %convolution_convert_fusion = bf16[256,1024]{1,0:T(8,128)(2,1)} fusion(bf16[256,2048]{1,0:T(8,128)(2,1)} %all-gather.10.cloned.1.call-done, bf16[2048,1024]{1,0:T(8,128)(2,1)} %all-gather.12.cloned.1.call-done), kind=kOutput, calls=%fused_computation.3 | convolution fusion | flops 1074003968 | bytes 5767168 | tf_op jit(solution)/shard_map/dot_general | solution.py:120
  (93 shorter events, 4.0 us)
Async XLA Ops:
  6.5 84.9 %copy-start = (bf16[128,128]{1,0:T(8,128)(2,1)S(1)}, bf16[128,128]{1,0:T(8,128)(2,1)}, u32[]{:S(2)}) copy-start(bf16[128,128]{1,0:T(8,128)(2,1)} %param.12) | copy-start | bytes 98308
  6.5 164.6 %all-gather.14.cloned.1.call-start = ((), (), s32[]{:S(2)}) async-start(), calls=%async_computation.3 | async-start | bytes 2162688 | tf_op jit(solution)/shard_map/all_gather | solution.py:19
  87.7 3.7 collective-permute-start
  93.1 166.9 %all-gather.8.cloned.1.call-start = ((), (), s32[]{:S(2)}) async-start(), calls=%async_computation | async-start | bytes 4325376 | tf_op jit(solution)/shard_map/all_gather | solution.py:64
  93.9 253.9 %all-gather.12.cloned.1.call-start = ((), (), s32[]{:S(2)}) async-start(), calls=%async_computation.2 | async-start | bytes 4325376 | tf_op jit(solution)/shard_map/all_gather | solution.py:122
  94.6 296.7 %all-gather.10.cloned.1.call-start = ((), (), s32[]{:S(2)}) async-start(), calls=%async_computation.1 | async-start | bytes 1114112 | tf_op jit(solution)/shard_map/all_gather | solution.py:118
  202.0 64.9 %copy-start.1 = (bf16[1,128,128]{2,1,0:T(8,128)(2,1)S(1)}, bf16[1,128,128]{2,1,0:T(8,128)(2,1)}, u32[]{:S(2)}) copy-start(bf16[1,128,128]{2,1,0:T(8,128)(2,1)} %param.11) | copy-start | bytes 98308
Sparse Core Ops, SparseCore 0:
  93.2 77.8 all-gather.13
  174.3 85.6 all-gather.7
  263.1 84.6 all-gather.11
  349.7 41.5 all-gather.9
where the time goes:
time: 404 us; the launch traced here: 402 us
  waiting for transfers between devices  224 us (55%)
  blocking collectives  111 us (27%)
  other arithmetic  30.2 us (7%)
  matrix products  21 us (5%)
  between operations  13.3 us (3%)
    all_gather x1, waiting for transfers between devices, per_device(): lax.all_gather(w_out, 'ctx', axis=0, tiled=True)  78.3 us
    all_gather x1, waiting for transfers between devices, per_device(): lax.all_gather(w_query, 'ctx', axis=0, tiled=True)  58 us
    all_gather x1, waiting for transfers between devices, per_device(): all_heads = lax.all_gather(attn_rows, 'head', axis=1, tiled=True)  43.5 us
    all_gather x1, waiting for transfers between devices, prefix(): lax.all_gather(part.astype(kind), axis)  41.1 us
    all_gather x1, blocking collectives, per_device(): lax.all_gather(w_keyval, 'ctx', axis=0, tiled=True)  39.9 us
    all_gather x1, blocking collectives, per_device(): lax.all_gather(pair_sum.astype(jnp.bfloat16), 'head', axis=1, tiled=True)  35.5 us
    all_gather x1, blocking collectives, prefix(): lax.all_gather(part.astype(kind), axis)  35.3 us
    select_n x64, other arithmetic, step(): return jax.tree.map(lambda a, b: jnp.where(reached, a, b), new, before)  29.3 us
  transfers between devices with their start and end apart: 5, of which 5 were waited for; matrix products, arithmetic and copies ran while one was open for 10% of the time, Pallas kernels for 0%

commit v1 on v0

--- a/solution.py
+++ b/solution.py
@@ -66,7 +66,9 @@
     )
     pair_sum = jnp.dot(
         columns,
-        lax.all_gather(w_keyval, "ctx", axis=0, tiled=True),
+        jnp.concatenate(
+            lax.all_to_all(jnp.stack([w_keyval] * lax.axis_size("ctx")), "ctx", 0, 0), axis=0
+        ),
         preferred_element_type=jnp.float32,
     )
     queries = query_sum.astype(jnp.bfloat16)

time: 404 us -> 380 us (0.941)
  blocking collectives: 111 us -> 59 us
  waiting for transfers between devices: 224 us -> 239 us
  starting transfers between devices: 2.53 us -> 13.2 us
    all_gather x1 -> x0, blocking collectives: 39.9 us -> none  [per_device(): lax.all_gather(w_keyval, 'ctx', axis=0, tiled=True)]
    all_to_all x0 -> x1, waiting for transfers between devices: none -> 16.2 us  [per_device(): lax.all_to_all(jnp.stack([w_keyval] * lax.axis_size('ctx')), 'ctx', 0, 0)]
    all_to_all x0 -> x1, starting transfers between devices: none -> 10.5 us  [per_device(): lax.all_to_all(jnp.stack([w_keyval] * lax.axis_size('ctx')), 'ctx', 0, 0)]
    all_gather x1, blocking collectives: 35.5 us -> 25.7 us  [per_device(): lax.all_gather(pair_sum.astype(jnp.bfloat16), 'head', axis=1, tiled=True)]
  transfers between devices with their start and end apart: 5 -> 6, of which waited for: 5 -> 6; matrix products, arithmetic and copies ran while one was open for 10% -> 10% of each run, Pallas kernels for 0% -> 0%
where the time goes in v1:
time: 380 us; the launch traced here: 379 us
  waiting for transfers between devices  239 us (63%)
  blocking collectives  59 us (16%)
  other arithmetic  30.2 us (8%)
  matrix products  21 us (6%)
  between operations  13.3 us (4%)
  starting transfers between devices  13.2 us (3%)
    all_gather x1, waiting for transfers between devices, per_device(): lax.all_gather(w_out, 'ctx', axis=0, tiled=True)  78.3 us
    all_gather x1, waiting for transfers between devices, per_device(): lax.all_gather(w_query, 'ctx', axis=0, tiled=True)  58 us
    all_gather x1, waiting for transfers between devices, per_device(): all_heads = lax.all_gather(attn_rows, 'head', axis=1, tiled=True)  43.5 us
    all_gather x1, waiting for transfers between devices, prefix(): lax.all_gather(part.astype(kind), axis)  40.6 us
    all_gather x1, blocking collectives, prefix(): lax.all_gather(part.astype(kind), axis)  33.3 us
    select_n x64, other arithmetic, step(): return jax.tree.map(lambda a, b: jnp.where(reached, a, b), new, before)  29.3 us
    all_gather x1, blocking collectives, per_device(): lax.all_gather(pair_sum.astype(jnp.bfloat16), 'head', axis=1, tiled=True)  25.7 us
    all_to_all x1, waiting for transfers between devices, per_device(): lax.all_to_all(jnp.stack([w_keyval] * lax.axis_size('ctx')), 'ctx', 0, 0)  16.2 us
  transfers between devices with their start and end apart: 6, of which 6 were waited for; matrix products, arithmetic and copies ran while one was open for 10% of the time, Pallas kernels for 0%

profile of v1, /device:TPU:1, one launch (start us, length us, event | category | flops | bytes accessed | tf_op | source)
XLA Modules:
  0.0 378.6 jit_solution(11672189682209694633)
XLA Ops:
  6.5 1.6 stack.2
  8.1 10.5 %all-to-all-start = ((bf16[32,512,16]{1,2,0:T(8,128)(2,1)}), bf16[32,512,16]{1,2,0:T(8,128)(2,1)S(1)}, u32[]{:S(2)}, u32[]{:S(2)}) async-start(bf16[32,512,16]{1,2,0:T(8,128)(2,1)} %stack.2), calls=%async_computation | async-start | bytes 1048576 | tf_op jit(solution)/shard_map/all_to_all | solution.py:70
  18.7 16.2 %all-to-all-done = bf16[32,512,16]{1,2,0:T(8,128)(2,1)S(1)} async-done(((bf16[32,512,16]{1,2,0:T(8,128)(2,1)}), bf16[32,512,16]{1,2,0:T(8,128)(2,1)S(1)}, u32[]{:S(2)}, u32[]{:S(2)}) %all-to-all-start) | async-done | bytes 524320 | tf_op jit(solution)/shard_map/all_to_all | solution.py:70
  34.9 5.6 %convolution_convert_fusion.3 = bf16[256,16]{0,1:T(8,128)(2,1)S(1)} fusion(bf16[256,16384]{1,0:T(8,128)(2,1)} %param.8, bf16[16384,16]{0,1:T(8,128)(2,1)S(1)} %bitcast.45), kind=kOutput, calls=%fused_computation.16 | convolution fusion | flops 134221824 | bytes 8921088 | tf_op jit(solution)/shard_map/dot_general | solution.py:67
  40.6 25.7 %all_gather.24 = bf16[256,256]{0,1:T(8,128)(2,1)S(1)} all-gather(bf16[256,16]{0,1:T(8,128)(2,1)S(1)} %convolution_convert_fusion.3), channel_id=1, replica_groups=mesh['ctx'=32,'head'=16] {'head'}, dimensions={1}, use_global_device_ids=true | all-gather | bytes 139264 | tf_op jit(solution)/shard_map/all_gather | solution.py:75
  66.4 2.5 collective-permute-start
  69.0 1.3 collective-permute-done
  73.6 33.3 %all-gather.2 = bf16[32,1,256]{2,1,0:T(2,128)(2,1)S(1)} all-gather(bf16[1,1,256]{2,1,0:T(2,128)(2,1)S(1)} %reshape.167), channel_id=3, replica_groups=mesh['ctx'=32,'head'=16] {'ctx'}, dimensions={0}, use_global_device_ids=true | all-gather | bytes 16896 | tf_op jit(solution)/shard_map/all_gather | solution.py:19
  106.9 40.6 %all-gather.14.cloned.1.call-done = bf16[8192,128]{1,0:T(8,128)(2,1)} async-done(((bf16[256,128]{1,0:T(8,128)(2,1)}), bf16[8192,128]{1,0:T(8,128)(2,1)}) %all-gather.14.cloned.1.call-update) | async-done | bytes 2097168 | tf_op jit(solution)/shard_map/all_gather | solution.py:19
  147.4 30.8 %while.16 = (s32[]{:T(128)}, f32[256,128]{1,0:T(8,128)S(1)}, f32[256]{0:T(256)S(1)}, s32[]{:T(128)}, bf16[32,256,128]{2,1,0:T(8,128)(2,1)}, /*index=5*/bf16[32,256]{1,0:T(8,128)(2,1)S(1)}, s32[]{:T(128)}, s32[]{:T(128)}) while((s32[]{:T(128)}, f32[256,128]{1,0:T(8,128)S(1)}, f32[256]{0:T(256)S(1)}, s32[]{:T(128)}, ...), condition=%wide.region_6.7_spmd.clone, body=%wide.region_5.6_spmd.clone.sunk | while | flops 132100 | bytes 332403 | solution.py:36
  147.4 0.9 add_select_fusion.4
  148.4 0.9 add_select_fusion.4
  149.3 0.9 add_select_fusion.4
  150.3 0.9 add_select_fusion.4
  151.3 0.9 add_select_fusion.4
  152.2 0.9 add_select_fusion.4
  153.2 0.9 add_select_fusion.4
  154.2 0.9 add_select_fusion.4
  155.1 0.9 add_select_fusion.4
  156.1 0.9 add_select_fusion.4
  157.1 0.9 add_select_fusion.4
  158.0 0.9 add_select_fusion.4
  159.0 0.9 add_select_fusion.4
  159.9 0.9 add_select_fusion.4
  160.9 0.9 add_select_fusion.4
  161.9 0.9 add_select_fusion.4
  162.8 0.9 add_select_fusion.4
  163.8 0.9 add_select_fusion.4
  164.8 0.9 add_select_fusion.4
  165.7 0.9 add_select_fusion.4
  166.7 0.9 add_select_fusion.4
  167.7 0.9 add_select_fusion.4
  168.6 0.9 add_select_fusion.4
  169.6 0.9 add_select_fusion.4
  170.6 0.9 add_select_fusion.4
  171.5 0.9 add_select_fusion.4
  172.5 0.9 add_select_fusion.4
  173.4 0.9 add_select_fusion.4
  174.4 0.9 add_select_fusion.4
  175.4 0.9 add_select_fusion.4
  176.3 0.9 add_select_fusion.4
  177.3 0.9 add_select_fusion.4
  178.3 58.0 %all-gather.8.cloned.1.call-done = bf16[16384,128]{1,0:T(8,128)(2,1)} async-done(((bf16[512,128]{1,0:T(8,128)(2,1)}), bf16[16384,128]{1,0:T(8,128)(2,1)}) %all-gather.8.cloned.1.call-update) | async-done | bytes 4194320 | tf_op jit(solution)/shard_map/all_gather | solution.py:64
  236.3 6.9 %convolution_convert_fusion.2 = bf16[256,128]{1,0:T(8,128)(2,1)S(1)} fusion(bf16[256,16384]{1,0:T(8,128)(2,1)} %param.8, bf16[16384,128]{1,0:T(8,128)(2,1)} %all-gather.8.cloned.1.call-done), kind=kOutput, calls=%fused_computation.15 | convolution fusion | flops 1073774592 | bytes 12648448 | tf_op jit(solution)/shard_map/dot_general | solution.py:62
  244.6 1.2 fusion.6
  245.8 78.3 %all-gather.12.cloned.1.call-done = bf16[2048,1024]{1,0:T(8,128)(2,1)} async-done(((bf16[64,1024]{1,0:T(8,128)(2,1)}), bf16[2048,1024]{1,0:T(8,128)(2,1)}) %all-gather.12.cloned.1.call-update) | async-done | bytes 4194320 | tf_op jit(solution)/shard_map/all_gather | solution.py:124
  324.1 43.5 %all-gather.10.cloned.1.call-done = bf16[256,2048]{1,0:T(8,128)(2,1)} async-done(((bf16[256,128]{1,0:T(8,128)(2,1)}), bf16[256,2048]{1,0:T(8,128)(2,1)}) %all-gather.10.cloned.1.call-update) | async-done | bytes 1048592 | tf_op jit(solution)/shard_map/all_gather | solution.py:120
  367.5 4.6 %convolution_convert_fusion = bf16[256,1024]{1,0:T(8,128)(2,1)} fusion(bf16[256,2048]{1,0:T(8,128)(2,1)} %all-gather.10.cloned.1.call-done, bf16[2048,1024]{1,0:T(8,128)(2,1)} %all-gather.12.cloned.1.call-done), kind=kOutput, calls=%fused_computation.3 | convolution fusion | flops 1074003968 | bytes 5767168 | tf_op jit(solution)/shard_map/dot_general | solution.py:122
  (96 shorter events, 5.7 us)
Async XLA Ops:
  6.5 63.7 %copy-start = (bf16[128,128]{1,0:T(8,128)(2,1)S(1)}, bf16[128,128]{1,0:T(8,128)(2,1)}, u32[]{:S(2)}) copy-start(bf16[128,128]{1,0:T(8,128)(2,1)} %param.12) | copy-start | bytes 98308
  8.1 26.8 %all-to-all-start = ((bf16[32,512,16]{1,2,0:T(8,128)(2,1)}), bf16[32,512,16]{1,2,0:T(8,128)(2,1)S(1)}, u32[]{:S(2)}, u32[]{:S(2)}) async-start(bf16[32,512,16]{1,2,0:T(8,128)(2,1)} %stack.2), calls=%async_computation | async-start | bytes 1048576 | tf_op jit(solution)/shard_map/all_to_all | solution.py:70
  18.6 128.8 %all-gather.14.cloned.1.call-start = ((), (), s32[]{:S(2)}) async-start(), calls=%async_computation.4 | async-start | bytes 2162688 | tf_op jit(solution)/shard_map/all_gather | solution.py:19
  66.4 3.9 %collective-permute-start = (bf16[64,256]{0,1:T(8,128)(2,1)S(1)}, bf16[64,256]{0,1:T(8,128)(2,1)S(1)}, u32[]{:S(2)}, u32[]{:S(2)}) collective-permute-start(bf16[64,256]{0,1:T(8,128)(2,1)S(1)} %slice.21), channel_id=1, source_target_pairs={{0,16},{16,32},{32,48},{48,64},{64,80},{80,96},{96,112},{112,128},... | collective-permute-start | bytes 98312 | tf_op jit(solution)/shard_map/ppermute | solution.py:13
  71.9 164.3 %all-gather.8.cloned.1.call-start = ((), (), s32[]{:S(2)}) async-start(), calls=%async_computation.1 | async-start | bytes 4325376 | tf_op jit(solution)/shard_map/all_gather | solution.py:64
  72.7 251.4 %all-gather.12.cloned.1.call-start = ((), (), s32[]{:S(2)}) async-start(), calls=%async_computation.3 | async-start | bytes 4325376 | tf_op jit(solution)/shard_map/all_gather | solution.py:124
  73.4 294.1 %all-gather.10.cloned.1.call-start = ((), (), s32[]{:S(2)}) async-start(), calls=%async_computation.2 | async-start | bytes 1114112 | tf_op jit(solution)/shard_map/all_gather | solution.py:120
  178.2 64.9 %copy-start.1 = (bf16[1,128,128]{2,1,0:T(8,128)(2,1)S(1)}, bf16[1,128,128]{2,1,0:T(8,128)(2,1)}, u32[]{:S(2)}) copy-start(bf16[1,128,128]{2,1,0:T(8,128)(2,1)} %param.11) | copy-start | bytes 98308
Sparse Core Ops, SparseCore 0:
  72.1 75.3 all-gather.13
  150.6 85.6 all-gather.7
  239.4 84.6 all-gather.11
  326.0 41.5 all-gather.9
